TPU v7x, 32 devices: a whole 2x2x4 slice. The times are simulated.
32 devices in a mesh: dp: 4 (over z), space: 2 (over core), mp: 4 (over y, x).
Axes of the slice: x: 2, y: 2, z: 4, core: 2. Of those that a mesh axis runs over, the one named last changes fastest.
Arguments:
- features: bfloat16 [64, 64, 1024], P(('dp', 'space'), None, 'mp'), parts along dimension 0, may hold values from -6 to 6
- deconv_weight: bfloat16 [4, 512, 1024], P(None, 'mp'), may hold values from -0.1875 to 0.1875
- deconv_bias: float32 [512], P('mp'), may hold values from -3 to 3
- lateral_eight: bfloat16 [256, 512], P('mp'), may hold values from -0.25 to 0.25
- lateral_coarse: bfloat16 [2, 256, 1024], P(None, 'mp'), may hold values from -0.1875 to 0.1875
- output_conv: bfloat16 [3, 256, 9, 256], P(None, 'mp'), may hold values from -0.125 to 0.125
- norm_gain: float32 [6, 256], replicated, may hold values from 0.1 to 1.9
- norm_shift: float32 [6, 256], replicated, may hold values from -3 to 3
Outputs:
- level_eight: bfloat16 [256, 16384], P('mp', ('dp', 'space')), parts along dimension 1
- level_sixteen: bfloat16 [256, 4096], P('mp', ('dp', 'space')), parts along dimension 1
- level_thirty: bfloat16 [256, 1024], P('mp', ('dp', 'space')), parts along dimension 1
- level_sixty: bfloat16 [256, 256], P('mp', ('dp', 'space')), parts along dimension 1
There are 4 independent parts, one for each index of `dp`. A program takes and returns all parts, laid end to end along the dimension named above; an argument that names none is the same for every part. Nothing has to cross between parts.
All inputs are finite; a program needn't handle non-finite values.
Results may differ from a plain program's by a relative error of at most 0.015.
Values may be sent and summed in bfloat16 or wider, within the bound.
A program may use at most 64 MiB of HBM per device.

v0:
```python
import jax
import jax.numpy as jnp
from jax import lax
from jax.sharding import PartitionSpec as P

EPSILON = 1e-06


def extended(block, sides, width):
    for axis, dim in sides:
        count = lax.axis_size(axis)
        forward = [(i, i + 1) for i in range(count - 1)]
        backward = [(target, source) for source, target in forward]
        low = lax.ppermute(
            lax.slice_in_dim(block, block.shape[dim] - width, None, axis=dim), axis, forward
        )
        high = lax.ppermute(lax.slice_in_dim(block, 0, width, axis=dim), axis, backward)
        block = jnp.concatenate([low, block, high], axis=dim)
    return block


def pool_pairs(values):
    height, width, depth = values.shape
    return jnp.max(values.reshape(height // 2, 2, width // 2, 2, depth), axis=(1, 3))


def contract_last(weight_rows, data):
    return lax.dot_general(
        weight_rows, data, (((1,), (1,)), ((), ())), preferred_element_type=jnp.float32
    )


def apply_norm(values, sums, squares, neck_width, gain_row, shift_row):
    floats = values.astype(jnp.float32)
    center = (sums / neck_width)[None, :]
    spread = (squares / neck_width)[None, :] - center * center
    scaled = (floats - center) * lax.rsqrt(spread + EPSILON)
    return (scaled * gain_row[:, None] + shift_row[:, None]).astype(jnp.bfloat16)


def cell_moments(values):
    floats = values.astype(jnp.float32)
    return (jnp.sum(floats, axis=0), jnp.sum(floats * floats, axis=0))


def conv_taps(totals, padded, weight, height, width):
    depth = padded.shape[0]
    for tap_index in range(9):
        row_off = tap_index // 3
        col_off = tap_index % 3
        window = padded[:, row_off : row_off + height, col_off : col_off + width].reshape(
            depth, height * width
        )
        rows_used = weight[:, tap_index, :]
        totals = totals + jnp.dot(rows_used, window, preferred_element_type=jnp.float32)
    return totals


def pyramid_level(lateral, height, width, level_index, output_conv, norm_gain, norm_shift):
    local_ch = lateral.shape[0]
    neck_width = local_ch * lax.axis_size("mp")
    own_first = lax.axis_index("mp") * local_ch
    weight = output_conv[level_index]
    initial = jnp.zeros((local_ch, height * width), jnp.float32)
    gathered = lax.all_gather(lateral, "mp", axis=0, tiled=True)
    sums, squares = cell_moments(gathered)
    normed = apply_norm(
        gathered, sums, squares, neck_width, norm_gain[2 * level_index], norm_shift[2 * level_index]
    )
    rimmed = extended(normed.reshape(neck_width, height, width), (("space", 1),), 1)
    padded = jnp.pad(rimmed, ((0, 0), (0, 0), (1, 1)))
    conv_out = conv_taps(initial, padded, weight, height, width)
    convolved = conv_out.astype(jnp.bfloat16)
    sums, squares = lax.psum(cell_moments(convolved), "mp")
    gain_row = lax.dynamic_slice_in_dim(norm_gain[2 * level_index + 1], own_first, local_ch, 0)
    shift_row = lax.dynamic_slice_in_dim(norm_shift[2 * level_index + 1], own_first, local_ch, 0)
    return apply_norm(convolved, sums, squares, neck_width, gain_row, shift_row)


def channel_pyramid(
    features,
    deconv_weight,
    deconv_bias,
    lateral_eight,
    lateral_coarse,
    output_conv,
    norm_gain,
    norm_shift,
):
    row_count, col_count, _ = features.shape
    half_local = deconv_weight.shape[1]
    neck_local = lateral_coarse.shape[1]
    pixels = row_count * col_count
    coarse_pixels = row_count // 2 * (col_count // 2)
    deconv_flat = deconv_weight.reshape(4 * half_local, deconv_weight.shape[2])
    piece = lax.all_gather(features, "mp", axis=2, tiled=True)
    depth = piece.shape[2]
    flattened = piece.reshape(pixels, depth)
    raised = contract_last(deconv_flat, flattened)
    middle = contract_last(lateral_coarse[0], flattened)
    pooled_flat = pool_pairs(piece).reshape(coarse_pixels, depth)
    coarse = contract_last(lateral_coarse[1], pooled_flat)
    raised, middle, coarse = (raised, middle, coarse)
    raised = (
        raised.reshape(2, 2, half_local, row_count, col_count)
        + deconv_bias[None, None, :, None, None]
    )
    upsampled = raised.transpose(2, 3, 0, 4, 1).reshape(half_local, 4 * pixels).astype(jnp.bfloat16)
    piece = lax.all_gather(upsampled, "mp", axis=0, tiled=True)
    lateral_sum = jnp.dot(lateral_eight, piece, preferred_element_type=jnp.float32)
    lat_eight = lateral_sum.astype(jnp.bfloat16)
    lat_sixteen = middle.astype(jnp.bfloat16)
    lat_thirty = coarse.astype(jnp.bfloat16)
    level_eight = pyramid_level(
        lat_eight, 2 * row_count, 2 * col_count, 0, output_conv, norm_gain, norm_shift
    )
    level_sixteen = pyramid_level(
        lat_sixteen, row_count, col_count, 1, output_conv, norm_gain, norm_shift
    )
    level_thirty = pyramid_level(
        lat_thirty, row_count // 2, col_count // 2, 2, output_conv, norm_gain, norm_shift
    )
    level_sixty = level_thirty.reshape(neck_local, row_count // 2, col_count // 2)[
        :, ::2, ::2
    ].reshape(neck_local, -1)
    return (level_eight, level_sixteen, level_thirty, level_sixty)


def per_device(
    features,
    deconv_weight,
    deconv_bias,
    lateral_eight,
    lateral_coarse,
    output_conv,
    norm_gain,
    norm_shift,
):
    return channel_pyramid(
        features,
        deconv_weight,
        deconv_bias,
        lateral_eight,
        lateral_coarse,
        output_conv,
        norm_gain,
        norm_shift,
    )


def solution(mesh):
    return jax.shard_map(
        per_device,
        mesh=mesh,
        in_specs=(
            P(("dp", "space"), None, "mp"),
            P(None, "mp", None),
            P("mp"),
            P("mp", None),
            P(None, "mp", None),
            P(None, "mp", None, None),
            P(),
            P(),
        ),
        out_specs=(
            P("mp", ("dp", "space")),
            P("mp", ("dp", "space")),
            P("mp", ("dp", "space")),
            P("mp", ("dp", "space")),
        ),
        check_vma=False,
    )
```

profile of v0, /device:TPU:0, one launch (start us, length us, event | category | flops | bytes accessed | tf_op | source)
XLA Modules:
  0.0 179.7 jit_solution(12206708031647192003)
XLA Ops:
  7.2 0.7 all-gather.4.cloned.1.call-update
  8.0 0.9 fusion.99
  8.9 0.9 fusion.100
  11.7 2.0 %slice_bitcast_fusion = (bf16[64,9,256]{2,0,1:T(8,128)(2,1)S(1)}, bf16[64,9,256]{2,0,1:T(8,128)(2,1)}, bf16[64,9,256]{2,0,1:T(8,128)(2,1)}) fusion(bf16[3,64,9,256]{3,1,2,0:T(8,128)(2,1)} %param.13), kind=kLoop, calls=%fused_computation.94 | loop fusion | bytes 1769472 | tf_op jit(solution)/shard_map/squeeze | solution.py:63
  13.8 25.2 %all-gather.4.cloned.1.call-done = bf16[8,64,1024]{2,1,0:T(8,128)(2,1)} async-done(((bf16[8,64,256]{2,1,0:T(8,128)(2,1)}), bf16[8,64,1024]{2,1,0:T(8,128)(2,1)}) %all-gather.4.cloned.1.call-update) | async-done | bytes 1048592 | tf_op jit(solution)/shard_map/all_gather | solution.py:96
  39.0 1.6 reshape.228
  40.5 2.5 %reduce_max.9 = bf16[4,32,1024]{2,1,0:T(8,128)(2,1)} reduce(bf16[4,2,32,2,1024]{4,3,2,1,0:T(2,128)(2,1)S(1)} %reshape.228, bf16[]{:T(256)} %constant.41.clone.1), dimensions={1,3}, to_apply=%region_12.13 | reduce | flops 393216 | bytes 1310722 | tf_op jit(solution)/shard_map/reduce_max | solution.py:24
  43.1 1.2 fusion.26
  44.3 8.2 %all_gather.19 = bf16[256,128]{1,0:T(8,128)(2,1)S(1)} all-gather(bf16[64,128]{1,0:T(8,128)(2,1)S(1)} %fusion.26), channel_id=1, replica_groups=mesh['dp'=4,'space'=2,'mp'=4] {'mp'}, dimensions={0}, use_global_device_ids=true | all-gather | bytes 81920 | tf_op jit(solution)/shard_map/all_gather | solution.py:65
  52.8 1.3 collective-permute-start.4
  54.1 1.3 collective-permute-start.5
  55.4 1.3 convolution_convert_fusion.1
  56.8 8.3 %all_gather.18 = bf16[256,512]{1,0:T(8,128)(2,1)S(1)} all-gather(bf16[64,512]{1,0:T(8,128)(2,1)S(1)} %convolution_convert_fusion.1), channel_id=1, replica_groups=mesh['dp'=4,'space'=2,'mp'=4] {'mp'}, dimensions={0}, use_global_device_ids=true | all-gather | bytes 327680 | tf_op jit(solution)/shard_map/all_gather | solution.py:65
  66.1 1.4 collective-permute-start.2
  67.6 1.3 collective-permute-start.3
  68.9 0.7 fusion.15
  69.7 1.3 copy.13
  72.5 0.7 fusion.92
  73.7 33.4 %all-gather.6.cloned.1.call-done = bf16[512,2048]{0,1:T(8,128)(2,1)} async-done(((bf16[128,2048]{0,1:T(8,128)(2,1)}), bf16[512,2048]{0,1:T(8,128)(2,1)}) %all-gather.6.cloned.1.call-update) | async-done | bytes 2097168 | tf_op jit(solution)/shard_map/all_gather | solution.py:109
  107.1 3.0 %fusion.8 = bf16[64,2048]{1,0:T(8,128)(2,1)} fusion(bf16[512,2048]{0,1:T(8,128)(2,1)} %all-gather.6.cloned.1.call-done, bf16[64,512]{1,0:T(8,128)(2,1)S(1)} %copy-done.5), kind=kOutput, calls=%fused_computation.22 | convolution fusion | flops 134348800 | bytes 2424832 | tf_op jit(solution)/shard_map/dot_general | solution.py:110
  111.7 25.2 %all-gather.8.cloned.1.call-done = bf16[256,2048]{1,0:T(8,128)(2,1)} async-done(((bf16[64,2048]{1,0:T(8,128)(2,1)}), bf16[256,2048]{1,0:T(8,128)(2,1)}) %all-gather.8.cloned.1.call-update) | async-done | bytes 1048592 | tf_op jit(solution)/shard_map/all_gather | solution.py:65
  136.8 1.5 convert_reduce_fusion
  138.4 1.7 fusion.89
  140.5 1.6 collective-permute-start
  142.1 1.5 collective-permute-start.1
  143.8 1.5 collective-permute-done.1
  145.4 2.9 %fusion.5 = bf16[256,18,130]{2,1,0:T(8,128)(2,1)S(1)} fusion(bf16[256,1,128]{2,1,0:T(2,128)(2,1)S(1)} %collective-permute-done.1, bf16[256,16,128]{2,1,0:T(8,128)(2,1)S(1)} %bitcast.224, bf16[256,1,128]{2,1,0:T(2,128)(2,1)S(1)} %collective-permute-done), kind=kLoop, calls=%fused_computation.7 | loop fusion | flops 7188480 | bytes 2377728 | tf_op jit(solution)/shard_map/concatenate | solution.py:18
  148.3 2.2 %fusion.93 = (bf16[256,16,128]{2,1,0:T(8,128)(2,1)S(1)}, bf16[256,16,128]{2,1,0:T(8,128)(2,1)S(1)}, bf16[256,16,128]{2,1,0:T(8,128)(2,1)S(1)}, bf16[256,16,128]{...) fusion(bf16[256,18,130]{2,1,0:T(8,128)(2,1)S(1)} %fusion.5), kind=kLoop, calls=%fused_computation.189 | loop fusion | bytes 12582912 | tf_op jit(solution)/shard_map/slice | solution.py:51
  150.8 1.1 pad_maximum_fusion
  155.3 15.3 %all-reduce.3 = (f32[2048]{0:T(1024)S(1)}, f32[2048]{0:T(1024)S(1)}, f32[512]{0:T(512)S(1)}, f32[512]{0:T(512)S(1)}, f32[128]{0:T(128)S(1)}, /*index=5*/f32[128]{0:T(128)S(1)}) all-reduce(f32[2048]{0:T(1024)S(1)} %get-tuple-element.7, f32[2048]{0:T(1024)S(1)} %get-tuple-element.6, ...), channel_id=1, replica_groups=mesh['dp'=4,'space'=2,'mp'=4] {'mp'}, use_global_device_ids=true, to_apply=%region_5.6 | all-reduce | flops 5376 | bytes 43008 | tf_op jit(solution)/shard_map/psum | solution.py:74
  171.6 0.7 fusion.72
  172.3 0.8 fusion.56
  (92 shorter events, 11.8 us)
Async XLA Ops:
  7.2 61.7 %copy-start = (bf16[4,128,1024]{2,1,0:T(8,128)(2,1)S(1)}, bf16[4,128,1024]{2,1,0:T(8,128)(2,1)}, u32[]{:S(2)}) copy-start(bf16[4,128,1024]{2,1,0:T(8,128)(2,1)} %param.9) | copy-start | bytes 3145732
  7.2 31.8 %all-gather.4.cloned.1.call-start = ((), (), s32[]{:S(2)}) async-start(), calls=%async_computation | async-start | bytes 1310720 | tf_op jit(solution)/shard_map/all_gather | solution.py:96
  7.9 99.2 %all-gather.6.cloned.1.call-start = ((), (), s32[]{:S(2)}) async-start(), calls=%async_computation.1 | async-start | bytes 2621440 | tf_op jit(solution)/shard_map/all_gather | solution.py:109
  39.0 16.5 %copy-start.2 = (bf16[8,64,1024]{2,1,0:T(8,128)(2,1)S(1)}, bf16[8,64,1024]{2,1,0:T(8,128)(2,1)}, u32[]{:S(2)}) copy-start(bf16[8,64,1024]{2,1,0:T(8,128)(2,1)} %all-gather.4.cloned.1.call-done) | copy-start | bytes 3145732
  43.1 25.9 %copy-start.13 = (f32[128]{0:T(128)S(1)}, f32[128]{0:T(128)}, u32[]{:S(2)}) copy-start(f32[128]{0:T(128)} %param.10) | copy-start | bytes 1540
  52.8 18.3 %collective-permute-start.4 = (bf16[256,1,32]{0,2,1:T(8,128)(2,1)S(1)}, bf16[256,1,32]{0,2,1:T(8,128)(2,1)S(1)}, u32[]{:S(2)}, u32[]{:S(2)}) collective-permute-start(bf16[256,1,32]{0,2,1:T(8,128)(2,1)S(1)} %get-tuple-element.53), channel_id=1, source_target_pairs={{0,4},{1,5},{2,6},{3,7},{8,12},{9,13},{10,14},{11,15},{16,20},{17,... | collective-permute-start | bytes 49160 | tf_op jit(solution)/shard_map/ppermute | solution.py:14
  54.1 17.0 %collective-permute-start.5 = (bf16[256,1,32]{0,2,1:T(8,128)(2,1)S(1)}, bf16[256,1,32]{0,2,1:T(8,128)(2,1)S(1)}, u32[]{:S(2)}, u32[]{:S(2)}) collective-permute-start(bf16[256,1,32]{0,2,1:T(8,128)(2,1)S(1)} %get-tuple-element.54), channel_id=1, source_target_pairs={{4,0},{5,1},{6,2},{7,3},{12,8},{13,9},{14,10},{15,11},{20,16},{21,... | collective-permute-start | bytes 49160 | tf_op jit(solution)/shard_map/ppermute | solution.py:17
  66.1 7.0 %collective-permute-start.2 = (bf16[256,1,64]{0,2,1:T(8,128)(2,1)}, bf16[256,1,64]{0,2,1:T(8,128)(2,1)S(1)}, u32[]{:S(2)}, u32[]{:S(2)}) collective-permute-start(bf16[256,1,64]{0,2,1:T(8,128)(2,1)} %get-tuple-element.43), channel_id=1, source_target_pairs={{0,4},{1,5},{2,6},{3,7},{8,12},{9,13},{10,14},{11,15},{16,20},{17,... | collective-permute-start | bytes 98312 | tf_op jit(solution)/shard_map/ppermute | solution.py:14
  67.6 5.6 %collective-permute-start.3 = (bf16[256,1,64]{0,2,1:T(8,128)(2,1)}, bf16[256,1,64]{0,2,1:T(8,128)(2,1)S(1)}, u32[]{:S(2)}, u32[]{:S(2)}) collective-permute-start(bf16[256,1,64]{0,2,1:T(8,128)(2,1)} %get-tuple-element.44), channel_id=1, source_target_pairs={{4,0},{5,1},{6,2},{7,3},{12,8},{13,9},{14,10},{15,11},{20,16},{21,... | collective-permute-start | bytes 98312 | tf_op jit(solution)/shard_map/ppermute | solution.py:17
  71.0 65.8 %all-gather.8.cloned.1.call-start = ((), (), s32[]{:S(2)}) async-start(), calls=%async_computation.2 | async-start | bytes 1310720 | tf_op jit(solution)/shard_map/all_gather | solution.py:65
  72.3 1.2 copy-start.3
  73.1 34.0 %copy-start.5 = (bf16[64,512]{1,0:T(8,128)(2,1)S(1)}, bf16[64,512]{1,0:T(8,128)(2,1)}, u32[]{:S(2)}) copy-start(bf16[64,512]{1,0:T(8,128)(2,1)} %param.11) | copy-start | bytes 196612
  140.5 3.3 %collective-permute-start = (bf16[256,1,128]{2,1,0:T(2,128)(2,1)S(1)}, bf16[256,1,128]{2,1,0:T(2,128)(2,1)S(1)}, u32[]{:S(2)}, u32[]{:S(2)}) collective-permute-start(bf16[256,1,128]{2,1,0:T(2,128)(2,1)S(1)} %get-tuple-element.30), channel_id=1, source_target_pairs={{0,4},{1,5},{2,6},{3,7},{8,12},{9,13},{10,14},{11,15},{16,20},{17,... | collective-permute-start | bytes 196616 | tf_op jit(solution)/shard_map/ppermute | solution.py:14
  142.1 3.2 %collective-permute-start.1 = (bf16[256,1,128]{2,1,0:T(2,128)(2,1)S(1)}, bf16[256,1,128]{2,1,0:T(2,128)(2,1)S(1)}, u32[]{:S(2)}, u32[]{:S(2)}) collective-permute-start(bf16[256,1,128]{2,1,0:T(2,128)(2,1)S(1)} %get-tuple-element.31), channel_id=1, source_target_pairs={{4,0},{5,1},{6,2},{7,3},{12,8},{13,9},{14,10},{15,11},{20,16},{21,... | collective-permute-start | bytes 196616 | tf_op jit(solution)/shard_map/ppermute | solution.py:17
  148.3 2.2 %copy-start.4 = (bf16[64,9,256]{2,0,1:T(8,128)(2,1)S(1)}, bf16[64,9,256]{2,0,1:T(8,128)(2,1)}, u32[]{:S(2)}) copy-start(bf16[64,9,256]{2,0,1:T(8,128)(2,1)} %get-tuple-element.33) | copy-start | bytes 884740
  152.2 1.2 copy-start.1
  154.6 0.7 copy-start.11
  154.6 0.7 copy-start.12
  154.6 16.0 %copy-start.9 = (f32[64]{0:T(128)S(1)}, f32[64]{0:T(128)}, u32[]{:S(2)}) copy-start(f32[64]{0:T(128)} %get-tuple-element.86) | copy-start | bytes 772
  154.7 16.0 %copy-start.10 = (f32[64]{0:T(128)S(1)}, f32[64]{0:T(128)}, u32[]{:S(2)}) copy-start(f32[64]{0:T(128)} %get-tuple-element.87) | copy-start | bytes 772
  154.7 16.9 %copy-start.7 = (f32[64]{0:T(128)S(1)}, f32[64]{0:T(128)}, u32[]{:S(2)}) copy-start(f32[64]{0:T(128)} %get-tuple-element.83) | copy-start | bytes 772
  154.7 16.9 %copy-start.8 = (f32[64]{0:T(128)S(1)}, f32[64]{0:T(128)}, u32[]{:S(2)}) copy-start(f32[64]{0:T(128)} %get-tuple-element.85) | copy-start | bytes 772
  170.8 2.4 %copy-start.6 = (bf16[64,128]{1,0:T(8,128)(2,1)}, bf16[64,128]{1,0:T(8,128)(2,1)S(1)}, u32[]{:S(2)}) copy-start(bf16[64,128]{1,0:T(8,128)(2,1)S(1)} %fusion.81) | copy-start | bytes 49156
Sparse Core Ops, SparseCore 0:
  9.8 29.1 all-gather.3
  71.2 35.9 all-gather.5
  110.3 26.4 all-gather.7
where the time goes:
time: 180 us
  waiting for transfers between devices  86.1 us (48%)
  blocking collectives  31.9 us (18%)
  between operations  14.3 us (8%)
  local copies, waits for them, and re-layouts  13.9 us (8%)
  matrix products  13 us (7%)
  other arithmetic  12.1 us (7%)
  starting transfers between devices  8.49 us (5%)
    all_gather x1, waiting for transfers between devices, channel_pyramid(): piece = lax.all_gather(upsampled, 'mp', axis=0, tiled=True)  33.4 us
    all_gather x1, waiting for transfers between devices, channel_pyramid(): piece = lax.all_gather(features, 'mp', axis=2, tiled=True)  25.2 us
    all_gather x1, waiting for transfers between devices, pyramid_level(): gathered = lax.all_gather(lateral, 'mp', axis=0, tiled=True)  25.2 us
    all_gather x2, blocking collectives, pyramid_level(): gathered = lax.all_gather(lateral, 'mp', axis=0, tiled=True)  16.6 us
    psum x1, blocking collectives, pyramid_level(): sums, squares = lax.psum(cell_moments(convolved), 'mp')  15.3 us
    dot_general x27, matrix products, conv_taps(): jnp.dot(rows_used, window, preferred_element_type=jnp.float32)  6.68 us
    ppermute x3, starting transfers between devices, extended(): lax.ppermute(lax.slice_in_dim(block, block.shape[dim] - width, None, axis...  4.31 us
    concatenate x6, other arithmetic, extended(): block = jnp.concatenate([low, block, high], axis=dim)  4.2 us
  transfers between devices with their start and end apart: 9, of which 4 were waited for; matrix products, arithmetic and copies ran while one was open for 8% of the time, Pallas kernels for 0%

commit v1 on v0

--- a/solution.py
+++ b/solution.py
@@ -93,7 +93,12 @@
     pixels = row_count * col_count
     coarse_pixels = row_count // 2 * (col_count // 2)
     deconv_flat = deconv_weight.reshape(4 * half_local, deconv_weight.shape[2])
-    piece = lax.all_gather(features, "mp", axis=2, tiled=True)
+    ring = [features]
+    for hop in range(3):
+        ring.append(lax.ppermute(ring[-1], "mp", [(dev, (dev + 1) % 4) for dev in range(4)]))
+    piece = jnp.roll(
+        jnp.concatenate(ring[::-1], axis=2), (lax.axis_index("mp") + 1) * ring[0].shape[2], axis=2
+    )
     depth = piece.shape[2]
     flattened = piece.reshape(pixels, depth)
     raised = contract_last(deconv_flat, flattened)

time: 180 us -> 151 us (0.84)
  waiting for transfers between devices: 86.1 us -> 45.5 us
  starting transfers between devices: 8.49 us -> 17 us
    all_gather x1, waiting for transfers between devices: 33.4 us -> 2.94 us  [channel_pyramid(): piece = lax.all_gather(upsampled, 'mp', axis=0, tiled=True)]
    all_gather x1 -> x0, waiting for transfers between devices: 25.2 us -> none  [channel_pyramid(): piece = lax.all_gather(features, 'mp', axis=2, tiled=True)]
    ppermute x0 -> x3, waiting for transfers between devices: none -> 16.8 us  [channel_pyramid(): lax.ppermute(ring[-1], 'mp', [(dev, (dev + 1) % 4) for dev in range(4)])]
    ppermute x3, starting transfers between devices: 4.31 us -> 9.28 us  [extended(): lax.ppermute(lax.slice_in_dim(block, block.shape[dim] - width, None, axis...]
    ppermute x0 -> x3, starting transfers between devices: none -> 3.81 us  [channel_pyramid(): lax.ppermute(ring[-1], 'mp', [(dev, (dev + 1) % 4) for dev in range(4)])]
    reshape x0 -> x1, local copies, waits for them, and re-layouts: none -> 2.86 us  [channel_pyramid(): raised.reshape(2, 2, half_local, row_count, col_count)]
  transfers between devices with their start and end apart: 9 -> 11, of which waited for: 4 -> 6; matrix products, arithmetic and copies ran while one was open for 8% -> 9% of each run, Pallas kernels for 0% -> 0%
where the time goes in v1:
time: 151 us
  waiting for transfers between devices  45.5 us (30%)
  blocking collectives  32.4 us (21%)
  starting transfers between devices  17 us (11%)
  local copies, waits for them, and re-layouts  15.3 us (10%)
  between operations  14.7 us (10%)
  matrix products  13 us (9%)
  other arithmetic  12.7 us (8%)
    all_gather x1, waiting for transfers between devices, pyramid_level(): gathered = lax.all_gather(lateral, 'mp', axis=0, tiled=True)  25.2 us
    all_gather x2, blocking collectives, pyramid_level(): gathered = lax.all_gather(lateral, 'mp', axis=0, tiled=True)  17.1 us
    ppermute x3, waiting for transfers between devices, channel_pyramid(): lax.ppermute(ring[-1], 'mp', [(dev, (dev + 1) % 4) for dev in range(4)])  16.8 us
    psum x1, blocking collectives, pyramid_level(): sums, squares = lax.psum(cell_moments(convolved), 'mp')  15.4 us
    ppermute x3, starting transfers between devices, extended(): lax.ppermute(lax.slice_in_dim(block, block.shape[dim] - width, None, axis...  9.28 us
    dot_general x27, matrix products, conv_taps(): jnp.dot(rows_used, window, preferred_element_type=jnp.float32)  6.68 us
    concatenate x6, other arithmetic, extended(): block = jnp.concatenate([low, block, high], axis=dim)  4.2 us
    ppermute x3, starting transfers between devices, extended(): lax.ppermute(lax.slice_in_dim(block, 0, width, axis=dim), axis, backward)  3.88 us
  transfers between devices with their start and end apart: 11, of which 6 were waited for; matrix products, arithmetic and copies ran while one was open for 9% of the time, Pallas kernels for 0%

profile of v1, /device:TPU:0, one launch (start us, length us, event | category | flops | bytes accessed | tf_op | source)
XLA Modules:
  0.0 150.7 jit_solution(5130454134014211410)
XLA Ops:
  7.2 3.0 %collective-permute-start = (bf16[8,64,256]{2,1,0:T(8,128)(2,1)}, bf16[8,64,256]{2,1,0:T(8,128)(2,1)S(1)}, u32[]{:S(2)}, u32[]{:S(2)}) collective-permute-start(bf16[8,64,256]{2,1,0:T(8,128)(2,1)} %param.8), channel_id=1, source_target_pairs={{0,1},{1,2},{2,3},{3,0},{4,5},{5,6},{6,7},{7,4},{8,9},{9,10},{10,1... | collective-permute-start | bytes 786440 | tf_op jit(solution)/shard_map/ppermute | solution.py:98
  10.3 0.9 fusion.100
  11.2 6.5 %collective-permute-done = bf16[8,64,256]{2,1,0:T(8,128)(2,1)S(1)} collective-permute-done((bf16[8,64,256]{2,1,0:T(8,128)(2,1)}, bf16[8,64,256]{2,1,0:T(8,128)(2,1)S(1)}, u32[]{:S(2)}, u32[]{:S(2)}) %collective-permute-start) | collective-permute-done | bytes 262176 | tf_op jit(solution)/shard_map/ppermute | solution.py:98
  17.7 0.8 collective-permute-start.1
  18.5 0.9 fusion.99
  20.7 5.4 %collective-permute-done.1 = bf16[8,64,256]{2,1,0:T(8,128)(2,1)S(1)} collective-permute-done((bf16[8,64,256]{2,1,0:T(8,128)(2,1)S(1)}, bf16[8,64,256]{2,1,0:T(8,128)(2,1)S(1)}, u32[]{:S(2)}, u32[]{:S(2)}) %collective-permute-start.1) | collective-permute-done | bytes 262176 | tf_op jit(solution)/shard_map/ppermute | solution.py:98
  26.8 2.0 %slice_bitcast_fusion = (bf16[64,9,256]{2,0,1:T(8,128)(2,1)S(1)}, bf16[64,9,256]{2,0,1:T(8,128)(2,1)}, bf16[64,9,256]{2,0,1:T(8,128)(2,1)}) fusion(bf16[3,64,9,256]{3,1,2,0:T(8,128)(2,1)} %param.13), kind=kLoop, calls=%fused_computation.95 | loop fusion | bytes 1769472 | tf_op jit(solution)/shard_map/squeeze | solution.py:63
  28.8 4.8 %collective-permute-done.2 = bf16[8,64,256]{2,1,0:T(8,128)(2,1)S(1)} collective-permute-done((bf16[8,64,256]{2,1,0:T(8,128)(2,1)S(1)}, bf16[8,64,256]{2,1,0:T(8,128)(2,1)S(1)}, u32[]{:S(2)}, u32[]{:S(2)}) %collective-permute-start.2) | collective-permute-done | bytes 262176 | tf_op jit(solution)/shard_map/ppermute | solution.py:98
  34.5 1.7 %convolution_bitcast_fusion = f32[512,512]{0,1:T(8,128)} fusion(bf16[512,1024]{1,0:T(8,128)(2,1)S(1)} %bitcast.224, bf16[512,1024]{1,0:T(8,128)(2,1)S(1)} %bitcast.220), kind=kOutput, calls=%fused_computation.28 | convolution fusion | flops 536870912 | bytes 3145728 | tf_op jit(solution)/shard_map/dot_general | solution.py:28
  36.2 2.9 %reshape.211 = f32[2,2,128,8,64]{2,1,0,4,3:T(2,128)} reshape(f32[512,512]{0,1:T(8,128)} %convolution_bitcast_fusion) | data formatting | bytes 2097152 | tf_op jit(solution)/shard_map/reshape | solution.py:110
  39.1 1.4 fusion.50
  40.4 1.4 copy.22
  41.9 1.3 fusion.19
  43.2 8.8 %all_gather.14 = bf16[256,512]{1,0:T(8,128)(2,1)S(1)} all-gather(bf16[64,512]{1,0:T(8,128)(2,1)S(1)} %fusion.19), channel_id=1, replica_groups=mesh['dp'=4,'space'=2,'mp'=4] {'mp'}, dimensions={0}, use_global_device_ids=true | all-gather | bytes 327680 | tf_op jit(solution)/shard_map/all_gather | solution.py:65
  52.4 1.8 %reduce_max.9 = bf16[4,32,1024]{2,1,0:T(8,128)(2,1)S(1)} reduce(bf16[4,2,32,2,1024]{4,3,2,1,0:T(2,128)(2,1)S(1)} %reshape.230, bf16[]{:T(256)} %constant.64.clone.1), dimensions={1,3}, to_apply=%region_12.13 | reduce | flops 393216 | bytes 1310722 | tf_op jit(solution)/shard_map/reduce_max | solution.py:24
  54.5 8.3 %all_gather.15 = bf16[256,128]{1,0:T(8,128)(2,1)S(1)} all-gather(bf16[64,128]{1,0:T(8,128)(2,1)S(1)} %fusion.25), channel_id=1, replica_groups=mesh['dp'=4,'space'=2,'mp'=4] {'mp'}, dimensions={0}, use_global_device_ids=true | all-gather | bytes 81920 | tf_op jit(solution)/shard_map/all_gather | solution.py:65
  63.1 1.3 collective-permute-start.8
  64.4 3.0 %collective-permute-start.7 = (bf16[256,1,32]{0,2,1:T(8,128)(2,1)S(1)}, bf16[256,1,32]{0,2,1:T(8,128)(2,1)S(1)}, u32[]{:S(2)}, u32[]{:S(2)}) collective-permute-start(bf16[256,1,32]{0,2,1:T(8,128)(2,1)S(1)} %get-tuple-element.53), channel_id=1, source_target_pairs={{0,4},{1,5},{2,6},{3,7},{8,12},{9,13},{10,14},{11,15},{16,20},{17,... | collective-permute-start | bytes 49160 | tf_op jit(solution)/shard_map/ppermute | solution.py:14
  67.4 1.3 collective-permute-start.6
  68.7 3.0 %collective-permute-start.5 = (bf16[256,1,64]{0,2,1:T(8,128)(2,1)S(1)}, bf16[256,1,64]{0,2,1:T(8,128)(2,1)S(1)}, u32[]{:S(2)}, u32[]{:S(2)}) collective-permute-start(bf16[256,1,64]{0,2,1:T(8,128)(2,1)S(1)} %get-tuple-element.43), channel_id=1, source_target_pairs={{0,4},{1,5},{2,6},{3,7},{8,12},{9,13},{10,14},{11,15},{16,20},{17,... | collective-permute-start | bytes 98312 | tf_op jit(solution)/shard_map/ppermute | solution.py:14
  74.3 2.9 %all-gather.3.cloned.1.call-done = bf16[512,2048]{0,1:T(8,128)(2,1)} async-done(((bf16[128,2048]{0,1:T(8,128)(2,1)}), bf16[512,2048]{0,1:T(8,128)(2,1)}) %all-gather.3.cloned.1.call-update) | async-done | bytes 2097168 | tf_op jit(solution)/shard_map/all_gather | solution.py:114
  77.3 3.0 %fusion.8 = bf16[64,2048]{1,0:T(8,128)(2,1)} fusion(bf16[512,2048]{0,1:T(8,128)(2,1)} %all-gather.3.cloned.1.call-done, bf16[64,512]{1,0:T(8,128)(2,1)S(1)} %copy-done.6), kind=kOutput, calls=%fused_computation.22 | convolution fusion | flops 134348800 | bytes 2424832 | tf_op jit(solution)/shard_map/dot_general | solution.py:115
  81.8 25.2 %all-gather.5.cloned.1.call-done = bf16[256,2048]{1,0:T(8,128)(2,1)} async-done(((bf16[64,2048]{1,0:T(8,128)(2,1)}), bf16[256,2048]{1,0:T(8,128)(2,1)}) %all-gather.5.cloned.1.call-update) | async-done | bytes 1048592 | tf_op jit(solution)/shard_map/all_gather | solution.py:65
  107.0 1.5 %convert_reduce_fusion = (f32[2048]{0:T(1024)S(1)}, f32[2048]{0:T(1024)S(1)}) fusion(bf16[256,2048]{1,0:T(8,128)(2,1)} %all-gather.5.cloned.1.call-done), kind=kLoop, calls=%fused_computation.10 | loop fusion | flops 2093056 | bytes 1064960 | tf_op jit(solution)/shard_map/reduce_sum | solution.py:43
  108.5 1.7 %fusion.89 = bf16[32,8,16,128]{3,1,2,0:T(8,128)(2,1)S(1)} fusion(f32[256]{0:T(256)S(1)} %bitcast.260, f32[256]{0:T(256)S(1)} %bitcast.262, f32[2048]{0:T(1024)S(1)} %get-tuple-element.70, f32[2048]{0:T(1024)S(1)} %get-tuple-element.69, bf16[256,2048]{1,0:T(8,128)(2,1)} %all-gather.5.cloned.1.call-done), kind=kLoop, calls=%fused_computation.195 | loop fusion | flops 3145728 | bytes 2115584
  110.7 1.3 collective-permute-start.4
  112.0 3.2 %collective-permute-start.3 = (bf16[256,1,128]{2,1,0:T(2,128)(2,1)S(1)}, bf16[256,1,128]{2,1,0:T(2,128)(2,1)S(1)}, u32[]{:S(2)}, u32[]{:S(2)}) collective-permute-start(bf16[256,1,128]{2,1,0:T(2,128)(2,1)S(1)} %get-tuple-element.30), channel_id=1, source_target_pairs={{0,4},{1,5},{2,6},{3,7},{8,12},{9,13},{10,14},{11,15},{16,20},{17,... | collective-permute-start | bytes 196616 | tf_op jit(solution)/shard_map/ppermute | solution.py:14
  116.0 2.9 %fusion.5 = bf16[256,18,130]{2,1,0:T(8,128)(2,1)S(1)} fusion(bf16[256,1,128]{2,1,0:T(2,128)(2,1)S(1)} %collective-permute-done.4, bf16[256,16,128]{2,1,0:T(8,128)(2,1)S(1)} %bitcast.222, bf16[256,1,128]{2,1,0:T(2,128)(2,1)S(1)} %collective-permute-done.3), kind=kLoop, calls=%fused_computation.7 | loop fusion | flops 7188480 | bytes 2377728 | tf_op jit(solution)/shard_map/concatenate | solution.py:18
  119.0 2.2 %fusion.93 = (bf16[256,16,128]{2,1,0:T(8,128)(2,1)S(1)}, bf16[256,16,128]{2,1,0:T(8,128)(2,1)S(1)}, bf16[256,16,128]{2,1,0:T(8,128)(2,1)S(1)}, bf16[256,16,128]{...) fusion(bf16[256,18,130]{2,1,0:T(8,128)(2,1)S(1)} %fusion.5), kind=kLoop, calls=%fused_computation.199 | loop fusion | bytes 12582912 | tf_op jit(solution)/shard_map/slice | solution.py:51
  121.5 1.1 pad_maximum_fusion
  126.0 15.4 %all-reduce.3 = (f32[2048]{0:T(1024)S(1)}, f32[2048]{0:T(1024)S(1)}, f32[512]{0:T(512)S(1)}, f32[512]{0:T(512)S(1)}, f32[128]{0:T(128)S(1)}, /*index=5*/f32[128]{0:T(128)S(1)}) all-reduce(f32[2048]{0:T(1024)S(1)} %get-tuple-element.7, f32[2048]{0:T(1024)S(1)} %get-tuple-element.6, ...), channel_id=1, replica_groups=mesh['dp'=4,'space'=2,'mp'=4] {'mp'}, use_global_device_ids=true, to_apply=%region_5.6 | all-reduce | flops 5376 | bytes 43008 | tf_op jit(solution)/shard_map/psum | solution.py:74
  142.3 0.8 fusion.56
  (108 shorter events, 14.1 us)
Async XLA Ops:
  7.2 27.3 %copy-start = (bf16[4,128,1024]{2,1,0:T(8,128)(2,1)S(1)}, bf16[4,128,1024]{2,1,0:T(8,128)(2,1)}, u32[]{:S(2)}) copy-start(bf16[4,128,1024]{2,1,0:T(8,128)(2,1)} %param.9) | copy-start | bytes 3145732
  7.2 26.5 %copy-start.4 = (bf16[8,64,256]{2,1,0:T(8,128)(2,1)S(1)}, bf16[8,64,256]{2,1,0:T(8,128)(2,1)}, u32[]{:S(2)}) copy-start(bf16[8,64,256]{2,1,0:T(8,128)(2,1)} %param.8) | copy-start | bytes 786436
  7.2 70.1 %all-gather.3.cloned.1.call-start = ((), (), s32[]{:S(2)}) async-start(), calls=%async_computation | async-start | bytes 2621440 | tf_op jit(solution)/shard_map/all_gather | solution.py:114
  7.2 10.5 %collective-permute-start = (bf16[8,64,256]{2,1,0:T(8,128)(2,1)}, bf16[8,64,256]{2,1,0:T(8,128)(2,1)S(1)}, u32[]{:S(2)}, u32[]{:S(2)}) collective-permute-start(bf16[8,64,256]{2,1,0:T(8,128)(2,1)} %param.8), channel_id=1, source_target_pairs={{0,1},{1,2},{2,3},{3,0},{4,5},{5,6},{6,7},{7,4},{8,9},{9,10},{10,1... | collective-permute-start | bytes 786440 | tf_op jit(solution)/shard_map/ppermute | solution.py:98
  17.7 8.4 %collective-permute-start.1 = (bf16[8,64,256]{2,1,0:T(8,128)(2,1)S(1)}, bf16[8,64,256]{2,1,0:T(8,128)(2,1)S(1)}, u32[]{:S(2)}, u32[]{:S(2)}) collective-permute-start(bf16[8,64,256]{2,1,0:T(8,128)(2,1)S(1)} %collective-permute-done), channel_id=1, source_target_pairs={{0,1},{1,2},{2,3},{3,0},{4,5},{5,6},{6,7},{7,4},{8,9},{9,10},{10,1... | collective-permute-start | bytes 786440 | tf_op jit(solution)/shard_map/ppermute | solution.py:98
  26.1 7.5 %collective-permute-start.2 = (bf16[8,64,256]{2,1,0:T(8,128)(2,1)S(1)}, bf16[8,64,256]{2,1,0:T(8,128)(2,1)S(1)}, u32[]{:S(2)}, u32[]{:S(2)}) collective-permute-start(bf16[8,64,256]{2,1,0:T(8,128)(2,1)S(1)} %collective-permute-done.1), channel_id=1, source_target_pairs={{0,1},{1,2},{2,3},{3,0},{4,5},{5,6},{6,7},{7,4},{8,9},{9,10},{10,1... | collective-permute-start | bytes 786440 | tf_op jit(solution)/shard_map/ppermute | solution.py:98
  34.5 4.6 %copy-start.14 = (f32[128]{0:T(128)S(1)}, f32[128]{0:T(128)}, u32[]{:S(2)}) copy-start(f32[128]{0:T(128)} %param.10) | copy-start | bytes 1540
  41.8 65.2 %all-gather.5.cloned.1.call-start = ((), (), s32[]{:S(2)}) async-start(), calls=%async_computation.1 | async-start | bytes 1310720 | tf_op jit(solution)/shard_map/all_gather | solution.py:65
  43.2 11.1 %copy-start.5 = (bf16[2,64,1024]{2,1,0:T(8,128)(2,1)S(1)}, bf16[2,64,1024]{2,1,0:T(8,128)(2,1)}, u32[]{:S(2)}) copy-start(bf16[2,64,1024]{2,1,0:T(8,128)(2,1)} %param.12) | copy-start | bytes 786436
  63.1 8.7 %collective-permute-start.8 = (bf16[256,1,32]{0,2,1:T(8,128)(2,1)S(1)}, bf16[256,1,32]{0,2,1:T(8,128)(2,1)S(1)}, u32[]{:S(2)}, u32[]{:S(2)}) collective-permute-start(bf16[256,1,32]{0,2,1:T(8,128)(2,1)S(1)} %get-tuple-element.54), channel_id=1, source_target_pairs={{4,0},{5,1},{6,2},{7,3},{12,8},{13,9},{14,10},{15,11},{20,16},{21,... | collective-permute-start | bytes 49160 | tf_op jit(solution)/shard_map/ppermute | solution.py:17
  64.4 7.4 %collective-permute-start.7 = (bf16[256,1,32]{0,2,1:T(8,128)(2,1)S(1)}, bf16[256,1,32]{0,2,1:T(8,128)(2,1)S(1)}, u32[]{:S(2)}, u32[]{:S(2)}) collective-permute-start(bf16[256,1,32]{0,2,1:T(8,128)(2,1)S(1)} %get-tuple-element.53), channel_id=1, source_target_pairs={{0,4},{1,5},{2,6},{3,7},{8,12},{9,13},{10,14},{11,15},{16,20},{17,... | collective-permute-start | bytes 49160 | tf_op jit(solution)/shard_map/ppermute | solution.py:14
  67.4 6.4 %collective-permute-start.6 = (bf16[256,1,64]{0,2,1:T(8,128)(2,1)S(1)}, bf16[256,1,64]{0,2,1:T(8,128)(2,1)S(1)}, u32[]{:S(2)}, u32[]{:S(2)}) collective-permute-start(bf16[256,1,64]{0,2,1:T(8,128)(2,1)S(1)} %get-tuple-element.44), channel_id=1, source_target_pairs={{4,0},{5,1},{6,2},{7,3},{12,8},{13,9},{14,10},{15,11},{20,16},{21,... | collective-permute-start | bytes 98312 | tf_op jit(solution)/shard_map/ppermute | solution.py:17
  68.7 5.1 %collective-permute-start.5 = (bf16[256,1,64]{0,2,1:T(8,128)(2,1)S(1)}, bf16[256,1,64]{0,2,1:T(8,128)(2,1)S(1)}, u32[]{:S(2)}, u32[]{:S(2)}) collective-permute-start(bf16[256,1,64]{0,2,1:T(8,128)(2,1)S(1)} %get-tuple-element.43), channel_id=1, source_target_pairs={{0,4},{1,5},{2,6},{3,7},{8,12},{9,13},{10,14},{11,15},{16,20},{17,... | collective-permute-start | bytes 98312 | tf_op jit(solution)/shard_map/ppermute | solution.py:14
  72.9 1.2 copy-start.2
  73.8 3.5 %copy-start.6 = (bf16[64,512]{1,0:T(8,128)(2,1)S(1)}, bf16[64,512]{1,0:T(8,128)(2,1)}, u32[]{:S(2)}) copy-start(bf16[64,512]{1,0:T(8,128)(2,1)} %param.11) | copy-start | bytes 196612
  110.7 4.8 %collective-permute-start.4 = (bf16[256,1,128]{2,1,0:T(2,128)(2,1)S(1)}, bf16[256,1,128]{2,1,0:T(2,128)(2,1)S(1)}, u32[]{:S(2)}, u32[]{:S(2)}) collective-permute-start(bf16[256,1,128]{2,1,0:T(2,128)(2,1)S(1)} %get-tuple-element.31), channel_id=1, source_target_pairs={{4,0},{5,1},{6,2},{7,3},{12,8},{13,9},{14,10},{15,11},{20,16},{21,... | collective-permute-start | bytes 196616 | tf_op jit(solution)/shard_map/ppermute | solution.py:17
  112.0 4.0 %collective-permute-start.3 = (bf16[256,1,128]{2,1,0:T(2,128)(2,1)S(1)}, bf16[256,1,128]{2,1,0:T(2,128)(2,1)S(1)}, u32[]{:S(2)}, u32[]{:S(2)}) collective-permute-start(bf16[256,1,128]{2,1,0:T(2,128)(2,1)S(1)} %get-tuple-element.30), channel_id=1, source_target_pairs={{0,4},{1,5},{2,6},{3,7},{8,12},{9,13},{10,14},{11,15},{16,20},{17,... | collective-permute-start | bytes 196616 | tf_op jit(solution)/shard_map/ppermute | solution.py:14
  118.9 2.2 %copy-start.3 = (bf16[64,9,256]{2,0,1:T(8,128)(2,1)S(1)}, bf16[64,9,256]{2,0,1:T(8,128)(2,1)}, u32[]{:S(2)}) copy-start(bf16[64,9,256]{2,0,1:T(8,128)(2,1)} %get-tuple-element.33) | copy-start | bytes 884740
  122.9 1.2 copy-start.1
  125.3 0.7 copy-start.12
  125.3 0.7 copy-start.13
  125.3 16.1 %copy-start.10 = (f32[64]{0:T(128)S(1)}, f32[64]{0:T(128)}, u32[]{:S(2)}) copy-start(f32[64]{0:T(128)} %get-tuple-element.86) | copy-start | bytes 772
  125.3 16.1 %copy-start.11 = (f32[64]{0:T(128)S(1)}, f32[64]{0:T(128)}, u32[]{:S(2)}) copy-start(f32[64]{0:T(128)} %get-tuple-element.87) | copy-start | bytes 772
  125.3 17.0 %copy-start.8 = (f32[64]{0:T(128)S(1)}, f32[64]{0:T(128)}, u32[]{:S(2)}) copy-start(f32[64]{0:T(128)} %get-tuple-element.82) | copy-start | bytes 772
  125.3 17.0 %copy-start.9 = (f32[64]{0:T(128)S(1)}, f32[64]{0:T(128)}, u32[]{:S(2)}) copy-start(f32[64]{0:T(128)} %get-tuple-element.84) | copy-start | bytes 772
  141.5 2.4 %copy-start.7 = (bf16[64,128]{1,0:T(8,128)(2,1)}, bf16[64,128]{1,0:T(8,128)(2,1)S(1)}, u32[]{:S(2)}) copy-start(bf16[64,128]{1,0:T(8,128)(2,1)S(1)} %fusion.81) | copy-start | bytes 49156
Sparse Core Ops, SparseCore 0:
  41.9 35.2 all-gather.2
  80.5 26.4 all-gather.4
